TPU v7x, 256 devices: a whole 4x4x8 slice. The times are simulated.
256 devices in a mesh: lat: 16 (over x, y), lon: 8 (over z), ens: 2 (over core).
Axes of the slice: x: 4, y: 4, z: 8, core: 2. Of those that a mesh axis runs over, the one named last changes fastest.
Arguments:
- parameters: float32 [2, 128, 128, 1024], P(None, 'ens', 'lat', 'lon'), may hold values from -1.2 to 1.2, as said below
- initial_height: float32 [128, 1024], P('lat', 'lon'), may hold values from -6 to 6
- initial_speed: float32 [2, 128, 1024], P(None, 'lat', 'lon'), may hold values from -4 to 4
- obs_slots: int32 [2, 128, 128, 8], P(None, ('lat', 'lon')), may hold values from -1 to 1023, as said below
- obs_values: float32 [2, 128, 128, 8], P(None, ('lat', 'lon')), may hold values from -6 to 6
- obs_precision: float32 [2, 128, 128, 8], P(None, ('lat', 'lon')), may hold values from 0 to 2, as said below
Outputs:
- calibrated: float32 [2, 128, 128, 1024], P(None, 'ens', 'lat', 'lon')
Inputs may be any that keep to these rules, and one draw needn't show every extreme that they name: `obs_slots`: for each iteration and owner, the live slots towards one receiver come first and name distinct cells of the owner's block (local index row * 128 + column); no cell is named twice by one owner in one iteration; in each iteration some receiving block has all 8 slots live from every owner. `obs_precision`: zero exactly where the matching slot of obs_slots (with receiver and owner swapped) is empty, 0.5 or more elsewhere. `parameters`: friction rates lie in 0.02 to 0.2, forcing in -1.2 to 1.2.
All inputs are finite; a program needn't handle non-finite values.
Results may differ from a plain program's by a relative error of at most 0.0003.
Values sent between devices are 32-bit elements; how exact they have to be, the bound alone decides.
No kernel may reach another device: no remote copies, remote signals or barrier semaphores. Data moves between devices by JAX's collectives and lax.ppermute only.
A program may use at most 64 MiB of HBM per device.

v0:
```python
import math
import jax
import jax.numpy as jnp
from jax import lax
from jax.sharding import Mesh
from jax.sharding import PartitionSpec as P

STEPS = 6
ITERS = 2
LAT = ("lat_0", "lat_1")
LAT_LON = ("lat_0", "lat_1", "lon")
depth_step = 0.7
gravity_step = 0.7
coriolis = 0.1


def padded_2(value, sides, width, wrap):
    for axis, dim in sides:
        peers, length = (lax.axis_size(axis), value.shape[dim])
        up = [(i, (i + 1) % peers) for i in range(peers if wrap else peers - 1)]
        down = [(j, i) for i, j in up]
        last = lax.slice_in_dim(value, length - width, length, axis=dim)
        leading = lax.slice_in_dim(value, 0, width, axis=dim)
        before = lax.ppermute(last, axis, up)
        after = lax.ppermute(leading, axis, down)
        value = jnp.concatenate([before, value, after], axis=dim)
    return value


def with_halo(value, sides, width):
    edges = {}
    for axis, dim in sides:
        peers, length = (lax.axis_size(axis), value.shape[dim])
        up = [(i, (i + 1) % peers) for i in range(peers)]
        last = lax.slice_in_dim(value, length - width, length, axis=dim)
        leading = lax.slice_in_dim(value, 0, width, axis=dim)
        edges[dim] = (
            lax.ppermute(last, axis, up),
            lax.ppermute(leading, axis, [(b, a) for a, b in up]),
        )
    done = []
    for _, dim in sides:
        low, high = edges[dim]
        around = [(width, width) if d in done else (0, 0) for d in range(value.ndim)]
        value = jnp.concatenate([jnp.pad(low, around), value, jnp.pad(high, around)], axis=dim)
        done.append(dim)
    return value


def in_one_piece(arrays, axis, split_dim, concat_dim, along):
    widths = [a.shape[along] for a in arrays]
    both = jnp.concatenate(arrays, axis=along)
    result = lax.all_to_all(both, axis, split_axis=split_dim, concat_axis=concat_dim, tiled=True)
    return tuple(jnp.split(result, [sum(widths[:k]) for k in range(1, len(widths))], axis=along))


def one_axis_at_a_time(value, axes):
    for axis in axes:
        value = lax.psum(value, axis)
    return value


def wall_rows(padded):
    row_count = padded.shape[-2]
    position = lax.axis_index(LAT)
    last_block = lax.axis_size(LAT) - 1
    row_ids = lax.broadcasted_iota(jnp.int32, (row_count, 1), 0)
    lower_wall = jnp.logical_and(row_ids == 0, position == 0)
    upper_wall = jnp.logical_and(row_ids == row_count - 1, position == last_block)
    keep_rows = jnp.logical_not(jnp.logical_or(lower_wall, upper_wall))
    return padded * keep_rows.astype(padded.dtype)


def advance(height, speeds, friction, forcing):
    east_padded = padded_2(speeds[0], (("lon", 2),), 1, True)
    north_padded = padded_2(speeds[1], ((LAT, 1),), 1, False)
    east_diff = east_padded[:, :, 2:] - east_padded[:, :, :-2]
    north_diff = north_padded[:, 2:, :] - north_padded[:, :-2, :]
    height = height - depth_step * (east_diff + north_diff) + forcing
    padded_height = with_halo(height, ((LAT, 1), ("lon", 2)), 1)
    padded_height = wall_rows(padded_height)
    slope_east = padded_height[:, 1:-1, 2:] - padded_height[:, 1:-1, :-2]
    slope_north = padded_height[:, 2:, 1:-1] - padded_height[:, :-2, 1:-1]
    eastward = (1.0 - friction) * speeds[0] - gravity_step * slope_east + coriolis * speeds[1]
    northward = (1.0 - friction) * speeds[1] - gravity_step * slope_north - coriolis * speeds[0]
    return (height, jnp.stack([eastward, northward]))


def forward(parameters, initial_height, initial_speed):
    members = parameters.shape[1]
    height = jnp.broadcast_to(initial_height, (members,) + initial_height.shape)
    speeds = jnp.broadcast_to(initial_speed[:, None], (2, members) + initial_height.shape)
    for substep in range(STEPS):
        height, speeds = advance(height, speeds, parameters[0], parameters[1])
    return height


def predict(height, cells):
    flattened = height.reshape(height.shape[0], -1)
    wanted = cells.reshape(-1)
    picked = jnp.take(flattened, jnp.clip(wanted, 0, flattened.shape[1] - 1), axis=1)
    picked = jnp.where(wanted[None, :] >= 0, picked, jnp.float32(0.0))
    return picked.T.reshape(cells.shape[0], -1)


def gram_terms(predicted, observed, precision):
    members = predicted.shape[1]
    centre = jnp.mean(predicted, axis=1, keepdims=True)
    spread = predicted - centre
    weighted = spread * precision[:, None]
    misfit = observed[:, None] - predicted
    gram_part = jnp.dot(spread.T, weighted, precision=lax.Precision.HIGHEST) / members
    cross_part = jnp.dot(weighted.T, misfit, precision=lax.Precision.HIGHEST) / math.sqrt(members)
    return (gram_part, cross_part)


def solve_weights(gram_part, cross_part):
    members = gram_part.shape[0]
    system = jnp.eye(members, dtype=jnp.float32) + gram_part
    factor = jnp.linalg.cholesky(system)
    weights = jax.scipy.linalg.cho_solve((factor, True), cross_part) / math.sqrt(members)
    return weights - jnp.mean(weights, axis=0, keepdims=True)


def per_device(parameters, initial_height, initial_speed, obs_slots, obs_values, obs_precision):
    owners = obs_slots.shape[2]
    slot_count = obs_slots.shape[3]
    members_here = parameters.shape[1]
    member_block = lax.axis_index("ens")
    owner_values, owner_precision = in_one_piece(
        (obs_values[:, 0], obs_precision[:, 0]), LAT_LON, 1, 1, 0
    )
    for iteration in range(ITERS):
        height = forward(parameters, initial_height, initial_speed)
        outgoing = predict(height, obs_slots[iteration, 0])
        received = outgoing
        observed = owner_values[iteration]
        precision = owner_precision[iteration]
        received = received.reshape(owners, slot_count, members_here)
        gathered = lax.all_gather(received, "ens", axis=2, tiled=True)
        members = gathered.shape[2]
        gram_part, cross_part = gram_terms(
            gathered.reshape(-1, members), observed.reshape(-1), precision.reshape(-1)
        )
        gram_part, cross_part = (
            one_axis_at_a_time(gram_part, LAT_LON),
            one_axis_at_a_time(cross_part, LAT_LON),
        )
        centred = solve_weights(gram_part, cross_part)
        local_weights = lax.dynamic_slice_in_dim(
            centred, member_block * members_here, members_here, 1
        )
        starting = jnp.zeros(
            (2, members_here, parameters.shape[2] * parameters.shape[3]), jnp.float32
        )
        pieces = lax.all_gather(parameters, "ens", axis=1, tiled=True)
        stacked = pieces.reshape(pieces.shape[0], pieces.shape[1], -1)
        increment = starting + jnp.einsum(
            "pjc,jm->pmc", stacked, local_weights, precision=lax.Precision.HIGHEST
        )
        parameters = parameters + increment.reshape(parameters.shape)
    return parameters


def solution(mesh):
    torus = Mesh(
        mesh.devices.reshape(4, 4, mesh.shape["lon"], mesh.shape["ens"]),
        ("lat_0", "lat_1", "lon", "ens"),
    )
    in_specs = (
        P(None, "ens", LAT, "lon"),
        P(LAT, "lon"),
        P(None, LAT, "lon"),
        P(None, LAT_LON, None, None),
        P(None, LAT_LON, None, None),
        P(None, LAT_LON, None, None),
    )
    out_specs = P(None, "ens", LAT, "lon")
    return jax.shard_map(
        per_device, mesh=torus, in_specs=in_specs, out_specs=out_specs, check_vma=False
    )
```

profile of v0, /device:TPU:2, one launch (start us, length us, event | category | flops | bytes accessed | tf_op | source)
XLA Modules:
  0.0 758.7 jit_solution(8578512216387290652)
XLA Ops:
  8.4 5.9 collective-permute-start
  14.5 4.9 collective-permute-start.2
  39.1 6.0 collective-permute-start.10
  49.3 4.3 collective-permute-done.8
  80.1 5.1 collective-permute-done.16
  99.3 8.5 %all-to-all-start = ((f32[4,128,8]{2,0,1:T(4,128)}), f32[4,128,8]{2,0,1:T(4,128)S(1)}, u32[]{:S(2)}, u32[]{:S(2)}) async-start(f32[4,128,8]{2,0,1:T(4,128)} %copy.61), calls=%async_computation | async-start | bytes 524288 | tf_op jit(solution)/shard_map/all_to_all | solution.py:53
  112.8 4.5 collective-permute-start.26
  140.1 5.8 collective-permute-start.34
  148.5 5.4 collective-permute-done.35
  169.9 6.1 collective-permute-start.42
  178.5 5.6 collective-permute-done.43
  193.8 43.5 %all-reduce.43.cloned.1.call-done = (f32[128,128]{1,0:T(8,128)}, f32[128,128]{0,1:T(8,128)}) async-done(((f32[128,128]{1,0:T(8,128)}, f32[128,128]{0,1:T(8,128)}), (f32[128,128]{1,0:T(8,128)}, f32[128,128]{0,1:T(8,128)})) %all-reduce.43.cloned.1.call-update) | async-done | bytes 131088 | tf_op jit(solution)/shard_map/psum | solution.py:59
  237.4 50.5 %all-reduce.39.cloned.1.call-done = (f32[128,128]{1,0:T(8,128)}, f32[128,128]{0,1:T(8,128)}) async-done(((f32[128,128]{1,0:T(8,128)}, f32[128,128]{0,1:T(8,128)}), (f32[128,128]{1,0:T(8,128)}, f32[128,128]{0,1:T(8,128)})) %all-reduce.39.cloned.1.call-update) | async-done | bytes 131088 | tf_op jit(solution)/shard_map/psum | solution.py:59
  288.5 74.1 %all-reduce.35.cloned.1.call-done = (f32[128,128]{1,0:T(8,128)}, f32[128,128]{0,1:T(8,128)}) async-done(((f32[128,128]{1,0:T(8,128)}, f32[128,128]{0,1:T(8,128)}), (f32[128,128]{1,0:T(8,128)}, f32[128,128]{0,1:T(8,128)})) %all-reduce.35.cloned.1.call-update) | async-done | bytes 131088 | tf_op jit(solution)/shard_map/psum | solution.py:59
  364.4 11.7 %cholesky.44 = f32[128,128]{1,0:T(8,128)S(1)} custom-call(f32[128,128]{1,0:T(8,128)S(1)} %fusion.178), custom_call_target="Cholesky" | custom-call | tf_op jit(solution)/shard_map/jit(cholesky)/cholesky | solution.py:120
  377.5 9.8 %custom-call.8 = f32[1,128,128]{1,2,0:T(8,128)S(1)} custom-call(f32[1,128,128]{2,1,0:T(8,128)S(1)} %fusion.163), custom_call_target="InvertDiagBlocksLowerTriangular" | custom-call | tf_op jit(solution)/shard_map/jit(_cho_solve)/triangular_solve | solution.py:121
  399.5 4.3 collective-permute-done.44
  418.2 4.5 collective-permute-done.49
  431.4 4.3 collective-permute-done.52
  448.2 4.3 collective-permute-done.56
  463.9 5.7 collective-permute-done.60
  479.0 4.3 collective-permute-done.64
  494.3 4.3 collective-permute-done.68
  499.8 4.5 collective-permute-start.74
  509.3 5.1 collective-permute-done.72
  530.3 6.0 collective-permute-start.82
  539.3 5.0 collective-permute-done.83
  552.9 43.8 %all-reduce.41.cloned.1.call-done = (f32[128,128]{1,0:T(8,128)}, f32[128,128]{0,1:T(8,128)}) async-done(((f32[128,128]{1,0:T(8,128)}, f32[128,128]{0,1:T(8,128)}), (f32[128,128]{1,0:T(8,128)}, f32[128,128]{0,1:T(8,128)})) %all-reduce.41.cloned.1.call-update) | async-done | bytes 131088 | tf_op jit(solution)/shard_map/psum | solution.py:59
  596.8 50.2 %all-reduce.37.cloned.1.call-done = (f32[128,128]{1,0:T(8,128)}, f32[128,128]{0,1:T(8,128)}) async-done(((f32[128,128]{1,0:T(8,128)}, f32[128,128]{0,1:T(8,128)}), (f32[128,128]{1,0:T(8,128)}, f32[128,128]{0,1:T(8,128)})) %all-reduce.37.cloned.1.call-update) | async-done | bytes 131088 | tf_op jit(solution)/shard_map/psum | solution.py:59
  647.6 74.1 %all-reduce.33.cloned.1.call-done = (f32[128,128]{1,0:T(8,128)}, f32[128,128]{0,1:T(8,128)}) async-done(((f32[128,128]{1,0:T(8,128)}, f32[128,128]{0,1:T(8,128)}), (f32[128,128]{1,0:T(8,128)}, f32[128,128]{0,1:T(8,128)})) %all-reduce.33.cloned.1.call-update) | async-done | bytes 131088 | tf_op jit(solution)/shard_map/psum | solution.py:59
  723.5 11.7 %cholesky.55 = f32[128,128]{1,0:T(8,128)S(1)} custom-call(f32[128,128]{1,0:T(8,128)S(1)} %fusion.174), custom_call_target="Cholesky" | custom-call | tf_op jit(solution)/shard_map/jit(cholesky)/cholesky | solution.py:120
  736.4 9.8 %custom-call.9 = f32[1,128,128]{1,2,0:T(8,128)S(1)} custom-call(f32[1,128,128]{2,1,0:T(8,128)S(1)} %fusion.164), custom_call_target="InvertDiagBlocksLowerTriangular" | custom-call | tf_op jit(solution)/shard_map/jit(_cho_solve)/triangular_solve | solution.py:121
  (348 shorter events, 248.0 us)
Async XLA Ops:
  8.4 13.0 %collective-permute-start = (f32[64,8,1]{2,1,0:T(8,128)S(1)}, f32[64,8,1]{2,1,0:T(8,128)S(1)}, u32[]{:S(2)}, u32[]{:S(2)}) collective-permute-start(f32[64,8,1]{2,1,0:T(8,128)S(1)} %broadcast_in_dim.78), channel_id=1, source_target_pairs={{2,0},{4,2},{6,4},{8,6},{10,8},{12,10},{14,12},{0,14},{3,1},{5,3},... | collective-permute-start | bytes 6152 | tf_op jit(solution)/shard_map/ppermute | solution.py:25
  39.1 17.7 %collective-permute-start.10 = (f32[64,1,128]{2,1,0:T(1,128)S(1)}, f32[64,1,128]{2,1,0:T(1,128)S(1)}, u32[]{:S(2)}, u32[]{:S(2)}) collective-permute-start(f32[64,1,128]{2,1,0:T(1,128)S(1)} %get-tuple-element.120), channel_id=1, source_target_pairs={{16,0},{32,16},{48,32},{64,48},{80,64},{96,80},{112,96},{128,112},... | collective-permute-start | bytes 98312 | tf_op jit(solution)/shard_map/ppermute | solution.py:25
  57.3 12.1 %collective-permute-start.13 = (f32[64,1,128]{2,1,0:T(1,128)S(1)}, f32[64,1,128]{2,1,0:T(1,128)S(1)}, u32[]{:S(2)}, u32[]{:S(2)}) collective-permute-start(f32[64,1,128]{2,1,0:T(1,128)S(1)} %get-tuple-element.114), channel_id=1, source_target_pairs={{0,16},{16,32},{32,48},{48,64},{64,80},{80,96},{96,112},{112,128},... | collective-permute-start | bytes 98312 | tf_op jit(solution)/shard_map/ppermute | solution.py:38
  57.4 12.0 %collective-permute-start.14 = (f32[64,1,128]{2,1,0:T(1,128)S(1)}, f32[64,1,128]{2,1,0:T(1,128)S(1)}, u32[]{:S(2)}, u32[]{:S(2)}) collective-permute-start(f32[64,1,128]{2,1,0:T(1,128)S(1)} %get-tuple-element.115), channel_id=1, source_target_pairs={{16,0},{32,16},{48,32},{64,48},{80,64},{96,80},{112,96},{128,112},... | collective-permute-start | bytes 98312 | tf_op jit(solution)/shard_map/ppermute | solution.py:39
  70.6 18.7 %collective-permute-start.18 = (f32[64,1,128]{2,1,0:T(1,128)S(1)}, f32[64,1,128]{2,1,0:T(1,128)S(1)}, u32[]{:S(2)}, u32[]{:S(2)}) collective-permute-start(f32[64,1,128]{2,1,0:T(1,128)S(1)} %get-tuple-element.112), channel_id=1, source_target_pairs={{16,0},{32,16},{48,32},{64,48},{80,64},{96,80},{112,96},{128,112},... | collective-permute-start | bytes 98312 | tf_op jit(solution)/shard_map/ppermute | solution.py:25
  74.4 14.8 %collective-permute-start.19 = (f32[64,1,128]{2,1,0:T(1,128)S(1)}, f32[64,1,128]{2,1,0:T(1,128)S(1)}, u32[]{:S(2)}, u32[]{:S(2)}) collective-permute-start(f32[64,1,128]{2,1,0:T(1,128)S(1)} %get-tuple-element.113), channel_id=1, source_target_pairs={{0,16},{16,32},{32,48},{48,64},{64,80},{80,96},{96,112},{112,128},... | collective-permute-start | bytes 98312 | tf_op jit(solution)/shard_map/ppermute | solution.py:24
  91.1 16.8 %collective-permute-start.20 = (f32[64,8,1]{2,1,0:T(8,128)}, f32[64,8,1]{2,1,0:T(8,128)S(1)}, u32[]{:S(2)}, u32[]{:S(2)}) collective-permute-start(f32[64,8,1]{2,1,0:T(8,128)} %get-tuple-element.108), channel_id=1, source_target_pairs={{0,2},{2,4},{4,6},{6,8},{8,10},{10,12},{12,14},{14,0},{1,3},{3,5},... | collective-permute-start | bytes 6152 | tf_op jit(solution)/shard_map/ppermute | solution.py:38
  91.1 16.8 %collective-permute-start.23 = (f32[64,8,1]{2,1,0:T(8,128)S(1)}, f32[64,8,1]{2,1,0:T(8,128)S(1)}, u32[]{:S(2)}, u32[]{:S(2)}) collective-permute-start(f32[64,8,1]{2,1,0:T(8,128)S(1)} %get-tuple-element.109), channel_id=1, source_target_pairs={{2,0},{4,2},{6,4},{8,6},{10,8},{12,10},{14,12},{0,14},{3,1},{5,3},... | collective-permute-start | bytes 6152 | tf_op jit(solution)/shard_map/ppermute | solution.py:39
  94.3 13.6 %collective-permute-start.21 = (f32[64,1,128]{2,1,0:T(1,128)}, f32[64,1,128]{2,1,0:T(1,128)S(1)}, u32[]{:S(2)}, u32[]{:S(2)}) collective-permute-start(f32[64,1,128]{2,1,0:T(1,128)} %get-tuple-element.106), channel_id=1, source_target_pairs={{0,16},{16,32},{32,48},{48,64},{64,80},{80,96},{96,112},{112,128},... | collective-permute-start | bytes 98312 | tf_op jit(solution)/shard_map/ppermute | solution.py:38
  94.6 13.3 %collective-permute-start.22 = (f32[64,1,128]{2,1,0:T(1,128)}, f32[64,1,128]{2,1,0:T(1,128)}, u32[]{:S(2)}, u32[]{:S(2)}) collective-permute-start(f32[64,1,128]{2,1,0:T(1,128)} %get-tuple-element.107), channel_id=1, source_target_pairs={{16,0},{32,16},{48,32},{64,48},{80,64},{96,80},{112,96},{128,112},... | collective-permute-start | bytes 98312 | tf_op jit(solution)/shard_map/ppermute | solution.py:39
  99.3 78.9 %all-to-all-start = ((f32[4,128,8]{2,0,1:T(4,128)}), f32[4,128,8]{2,0,1:T(4,128)S(1)}, u32[]{:S(2)}, u32[]{:S(2)}) async-start(f32[4,128,8]{2,0,1:T(4,128)} %copy.61), calls=%async_computation | async-start | bytes 524288 | tf_op jit(solution)/shard_map/all_to_all | solution.py:53
  107.8 129.5 %all-reduce.43.cloned.1.call-start = ((), (), s32[]{:S(2)}) async-start(), calls=%async_computation.8 | async-start | bytes 262144 | tf_op jit(solution)/shard_map/psum | solution.py:59
  193.8 94.1 %all-reduce.39.cloned.1.call-start = ((), (), s32[]{:S(2)}) async-start(), calls=%async_computation.6 | async-start | bytes 262144 | tf_op jit(solution)/shard_map/psum | solution.py:59
  237.3 125.3 %all-reduce.35.cloned.1.call-start = ((), (), s32[]{:S(2)}) async-start(), calls=%async_computation.4 | async-start | bytes 262144 | tf_op jit(solution)/shard_map/psum | solution.py:59
  287.9 100.0 %all-gather.3.cloned.1.call-start = ((), (), s32[]{:S(2)}) async-start(), calls=%async_computation.1 | async-start | bytes 1572864 | tf_op jit(solution)/shard_map/all_gather | solution.py:156
  288.5 308.2 %all-reduce.41.cloned.1.call-start = ((), (), s32[]{:S(2)}) async-start(), calls=%async_computation.7 | async-start | bytes 262144 | tf_op jit(solution)/shard_map/psum | solution.py:59
  391.5 12.6 %collective-permute-start.45 = (f32[64,1,128]{2,1,0:T(1,128)S(1)}, f32[64,1,128]{2,1,0:T(1,128)S(1)}, u32[]{:S(2)}, u32[]{:S(2)}) collective-permute-start(f32[64,1,128]{2,1,0:T(1,128)S(1)} %get-tuple-element.82), channel_id=1, source_target_pairs={{0,16},{16,32},{32,48},{48,64},{64,80},{80,96},{96,112},{112,128},... | collective-permute-start | bytes 98312 | tf_op jit(solution)/shard_map/ppermute | solution.py:38
  405.2 17.5 %collective-permute-start.50 = (f32[64,1,128]{2,1,0:T(1,128)S(1)}, f32[64,1,128]{2,1,0:T(1,128)S(1)}, u32[]{:S(2)}, u32[]{:S(2)}) collective-permute-start(f32[64,1,128]{2,1,0:T(1,128)S(1)} %get-tuple-element.80), channel_id=1, source_target_pairs={{16,0},{32,16},{48,32},{64,48},{80,64},{96,80},{112,96},{128,112},... | collective-permute-start | bytes 98312 | tf_op jit(solution)/shard_map/ppermute | solution.py:25
  407.7 15.0 %collective-permute-start.51 = (f32[64,1,128]{2,1,0:T(1,128)S(1)}, f32[64,1,128]{2,1,0:T(1,128)S(1)}, u32[]{:S(2)}, u32[]{:S(2)}) collective-permute-start(f32[64,1,128]{2,1,0:T(1,128)S(1)} %get-tuple-element.81), channel_id=1, source_target_pairs={{0,16},{16,32},{32,48},{48,64},{64,80},{80,96},{96,112},{112,128},... | collective-permute-start | bytes 98312 | tf_op jit(solution)/shard_map/ppermute | solution.py:24
  423.3 14.0 %collective-permute-start.53 = (f32[64,1,128]{2,1,0:T(1,128)S(1)}, f32[64,1,128]{2,1,0:T(1,128)S(1)}, u32[]{:S(2)}, u32[]{:S(2)}) collective-permute-start(f32[64,1,128]{2,1,0:T(1,128)S(1)} %get-tuple-element.74), channel_id=1, source_target_pairs={{0,16},{16,32},{32,48},{48,64},{64,80},{80,96},{96,112},{112,128},... | collective-permute-start | bytes 98312 | tf_op jit(solution)/shard_map/ppermute | solution.py:38
  425.2 12.1 %collective-permute-start.54 = (f32[64,1,128]{2,1,0:T(1,128)S(1)}, f32[64,1,128]{2,1,0:T(1,128)S(1)}, u32[]{:S(2)}, u32[]{:S(2)}) collective-permute-start(f32[64,1,128]{2,1,0:T(1,128)S(1)} %get-tuple-element.75), channel_id=1, source_target_pairs={{16,0},{32,16},{48,32},{64,48},{80,64},{96,80},{112,96},{128,112},... | collective-permute-start | bytes 98312 | tf_op jit(solution)/shard_map/ppermute | solution.py:39
  438.4 17.3 %collective-permute-start.58 = (f32[64,1,128]{2,1,0:T(1,128)S(1)}, f32[64,1,128]{2,1,0:T(1,128)S(1)}, u32[]{:S(2)}, u32[]{:S(2)}) collective-permute-start(f32[64,1,128]{2,1,0:T(1,128)S(1)} %get-tuple-element.72), channel_id=1, source_target_pairs={{16,0},{32,16},{48,32},{64,48},{80,64},{96,80},{112,96},{128,112},... | collective-permute-start | bytes 98312 | tf_op jit(solution)/shard_map/ppermute | solution.py:25
  441.1 14.6 %collective-permute-start.59 = (f32[64,1,128]{2,1,0:T(1,128)S(1)}, f32[64,1,128]{2,1,0:T(1,128)S(1)}, u32[]{:S(2)}, u32[]{:S(2)}) collective-permute-start(f32[64,1,128]{2,1,0:T(1,128)S(1)} %get-tuple-element.73), channel_id=1, source_target_pairs={{0,16},{16,32},{32,48},{48,64},{64,80},{80,96},{96,112},{112,128},... | collective-permute-start | bytes 98312 | tf_op jit(solution)/shard_map/ppermute | solution.py:24
  456.1 13.5 %collective-permute-start.61 = (f32[64,1,128]{2,1,0:T(1,128)S(1)}, f32[64,1,128]{2,1,0:T(1,128)S(1)}, u32[]{:S(2)}, u32[]{:S(2)}) collective-permute-start(f32[64,1,128]{2,1,0:T(1,128)S(1)} %get-tuple-element.66), channel_id=1, source_target_pairs={{0,16},{16,32},{32,48},{48,64},{64,80},{80,96},{96,112},{112,128},... | collective-permute-start | bytes 98312 | tf_op jit(solution)/shard_map/ppermute | solution.py:38
  456.3 13.3 %collective-permute-start.62 = (f32[64,1,128]{2,1,0:T(1,128)S(1)}, f32[64,1,128]{2,1,0:T(1,128)S(1)}, u32[]{:S(2)}, u32[]{:S(2)}) collective-permute-start(f32[64,1,128]{2,1,0:T(1,128)S(1)} %get-tuple-element.67), channel_id=1, source_target_pairs={{16,0},{32,16},{48,32},{64,48},{80,64},{96,80},{112,96},{128,112},... | collective-permute-start | bytes 98312 | tf_op jit(solution)/shard_map/ppermute | solution.py:39
  470.7 15.6 %collective-permute-start.66 = (f32[64,1,128]{2,1,0:T(1,128)S(1)}, f32[64,1,128]{2,1,0:T(1,128)S(1)}, u32[]{:S(2)}, u32[]{:S(2)}) collective-permute-start(f32[64,1,128]{2,1,0:T(1,128)S(1)} %get-tuple-element.64), channel_id=1, source_target_pairs={{16,0},{32,16},{48,32},{64,48},{80,64},{96,80},{112,96},{128,112},... | collective-permute-start | bytes 98312 | tf_op jit(solution)/shard_map/ppermute | solution.py:25
  486.7 12.0 %collective-permute-start.69 = (f32[64,1,128]{2,1,0:T(1,128)S(1)}, f32[64,1,128]{2,1,0:T(1,128)S(1)}, u32[]{:S(2)}, u32[]{:S(2)}) collective-permute-start(f32[64,1,128]{2,1,0:T(1,128)S(1)} %get-tuple-element.58), channel_id=1, source_target_pairs={{0,16},{16,32},{32,48},{48,64},{64,80},{80,96},{96,112},{112,128},... | collective-permute-start | bytes 98312 | tf_op jit(solution)/shard_map/ppermute | solution.py:38
  499.8 16.9 %collective-permute-start.74 = (f32[64,1,128]{2,1,0:T(1,128)S(1)}, f32[64,1,128]{2,1,0:T(1,128)S(1)}, u32[]{:S(2)}, u32[]{:S(2)}) collective-permute-start(f32[64,1,128]{2,1,0:T(1,128)S(1)} %get-tuple-element.56), channel_id=1, source_target_pairs={{16,0},{32,16},{48,32},{64,48},{80,64},{96,80},{112,96},{128,112},... | collective-permute-start | bytes 98312 | tf_op jit(solution)/shard_map/ppermute | solution.py:25
  504.3 12.4 %collective-permute-start.75 = (f32[64,1,128]{2,1,0:T(1,128)S(1)}, f32[64,1,128]{2,1,0:T(1,128)S(1)}, u32[]{:S(2)}, u32[]{:S(2)}) collective-permute-start(f32[64,1,128]{2,1,0:T(1,128)S(1)} %get-tuple-element.57), channel_id=1, source_target_pairs={{0,16},{16,32},{32,48},{48,64},{64,80},{80,96},{96,112},{112,128},... | collective-permute-start | bytes 98312 | tf_op jit(solution)/shard_map/ppermute | solution.py:24
  552.9 94.1 %all-reduce.37.cloned.1.call-start = ((), (), s32[]{:S(2)}) async-start(), calls=%async_computation.5 | async-start | bytes 262144 | tf_op jit(solution)/shard_map/psum | solution.py:59
  596.8 125.0 %all-reduce.33.cloned.1.call-start = ((), (), s32[]{:S(2)}) async-start(), calls=%async_computation.3 | async-start | bytes 262144 | tf_op jit(solution)/shard_map/psum | solution.py:59
  647.0 99.8 %all-gather.5.cloned.1.call-start = ((), (), s32[]{:S(2)}) async-start(), calls=%async_computation.2 | async-start | bytes 1572864 | tf_op jit(solution)/shard_map/all_gather | solution.py:156
  (77 other events, 738.3 us)
Sparse Core Ops, SparseCore 0:
  193.9 43.3 all-reduce.42
  239.8 48.0 all-reduce.38
  290.2 72.3 all-reduce.34
  553.0 43.6 all-reduce.40
  599.0 48.0 all-reduce.36
  649.3 72.3 all-reduce.32
Sparse Core Ops, SparseCore 1:
  290.2 14.7 all-gather.2
  649.5 14.7 all-gather.4
where the time goes:
time: 768 us; the launch traced here: 759 us
  waiting for transfers between devices  443 us (58%)
  starting transfers between devices  194 us (25%)
  other arithmetic  68.4 us (9%)
  local copies, waits for them, and re-layouts  25.4 us (3%)
  between operations  16.6 us (2%)
    psum x6, waiting for transfers between devices, one_axis_at_a_time(): value = lax.psum(value, axis)  336 us
    ppermute x22, starting transfers between devices, padded_2(): after = lax.ppermute(leading, axis, down)  82.6 us
    ppermute x20, starting transfers between devices, with_halo(): lax.ppermute(leading, axis, [(b, a) for a, b in up])  69 us
    ppermute x22, waiting for transfers between devices, padded_2(): before = lax.ppermute(last, axis, up)  48.1 us
    ppermute x20, waiting for transfers between devices, with_halo(): lax.ppermute(last, axis, up)  28.7 us
    ppermute x22, waiting for transfers between devices, padded_2(): after = lax.ppermute(leading, axis, down)  27.1 us
    ppermute x22, starting transfers between devices, padded_2(): before = lax.ppermute(last, axis, up)  25.1 us
    another operation x6, other arithmetic, solve_weights(): factor = jnp.linalg.cholesky(system)  24.7 us
  transfers between devices with their start and end apart: 93, of which 38 were waited for; matrix products, arithmetic and copies ran while one was open for 8% of the time, Pallas kernels for 0%

commit v1 on v0

--- a/solution.py
+++ b/solution.py
@@ -56,7 +56,7 @@
 
 def one_axis_at_a_time(value, axes):
     for axis in axes:
-        value = lax.psum(value, axis)
+        value = jnp.sum(lax.all_gather(value, axis), axis=0)
     return value
 
 

time: 768 us -> 625 us (0.81)
  waiting for transfers between devices: 443 us -> 110 us
  blocking collectives: 4.37 us -> 205 us
    psum x6 -> x0, waiting for transfers between devices: 336 us -> none  [one_axis_at_a_time(): value = lax.psum(value, axis)]
    all_gather x0 -> x12, blocking collectives: none -> 201 us  [one_axis_at_a_time(): value = jnp.sum(lax.all_gather(value, axis), axis=0)]
  transfers between devices with their start and end apart: 93 -> 87, of which waited for: 38 -> 32; matrix products, arithmetic and copies ran while one was open for 8% -> 12% of each run, Pallas kernels for 0% -> 0%
where the time goes in v1:
time: 625 us; the launch traced here: 615 us
  blocking collectives  205 us (33%)
  starting transfers between devices  192 us (31%)
  waiting for transfers between devices  110 us (18%)
  other arithmetic  67.1 us (11%)
  local copies, waits for them, and re-layouts  21.2 us (3%)
  between operations  15.2 us (2%)
    all_gather x12, blocking collectives, one_axis_at_a_time(): value = jnp.sum(lax.all_gather(value, axis), axis=0)  201 us
    ppermute x22, starting transfers between devices, padded_2(): after = lax.ppermute(leading, axis, down)  78.7 us
    ppermute x20, starting transfers between devices, with_halo(): lax.ppermute(leading, axis, [(b, a) for a, b in up])  70.8 us
    ppermute x22, waiting for transfers between devices, padded_2(): before = lax.ppermute(last, axis, up)  49.8 us
    ppermute x22, waiting for transfers between devices, padded_2(): after = lax.ppermute(leading, axis, down)  28.7 us
    ppermute x20, waiting for transfers between devices, with_halo(): lax.ppermute(last, axis, up)  28.5 us
    ppermute x22, starting transfers between devices, padded_2(): before = lax.ppermute(last, axis, up)  28.1 us
    another operation x6, other arithmetic, solve_weights(): factor = jnp.linalg.cholesky(system)  24.9 us
  transfers between devices with their start and end apart: 87, of which 32 were waited for; matrix products, arithmetic and copies ran while one was open for 12% of the time, Pallas kernels for 0%

profile of v1, /device:TPU:2, one launch (start us, length us, event | category | flops | bytes accessed | tf_op | source)
XLA Modules:
  0.0 615.3 jit_solution(10529267531389008290)
XLA Ops:
  7.5 5.9 collective-permute-start
  13.7 4.9 collective-permute-start.2
  38.2 6.0 collective-permute-start.10
  79.3 5.8 collective-permute-done.16
  96.9 8.5 %all-to-all-start = ((f32[4,128,8]{2,0,1:T(4,128)}), f32[4,128,8]{2,0,1:T(4,128)S(1)}, u32[]{:S(2)}, u32[]{:S(2)}) async-start(f32[4,128,8]{2,0,1:T(4,128)} %copy.90), calls=%async_computation | async-start | bytes 524288 | tf_op jit(solution)/shard_map/all_to_all | solution.py:53
  110.3 4.5 collective-permute-start.26
  137.7 5.8 collective-permute-start.34
  146.1 5.4 collective-permute-done.35
  166.7 6.1 collective-permute-start.42
  175.3 5.6 collective-permute-done.43
  188.7 13.1 %all-gather = f32[512,128]{1,0:T(8,128)S(1)} all-gather(f32[128,128]{1,0:T(8,128)S(1)} %fusion.3), channel_id=2, replica_groups=mesh['lat_0'=4,'lat_1'=4,'lon'=8,'ens'=2] {'lat_0'}, dimensions={0}, use_global_device_ids=true | all-gather | bytes 327680 | tf_op jit(solution)/shard_map/all_gather | solution.py:59
  201.8 12.3 %all-gather.1 = f32[512,128]{1,0:T(8,128)S(1)} all-gather(f32[128,128]{1,0:T(8,128)S(1)} %reduce_sum.145), channel_id=3, replica_groups=mesh['lat_0'=4,'lat_1'=4,'lon'=8,'ens'=2] {'lat_1'}, dimensions={0}, use_global_device_ids=true | all-gather | bytes 327680 | tf_op jit(solution)/shard_map/all_gather | solution.py:59
  214.1 25.3 %all-gather.2 = f32[1024,128]{1,0:T(8,128)S(1)} all-gather(f32[128,128]{1,0:T(8,128)S(1)} %reduce_sum.146), channel_id=4, replica_groups=mesh['lat_0'=4,'lat_1'=4,'lon'=8,'ens'=2] {'lon'}, dimensions={0}, use_global_device_ids=true | all-gather | bytes 589824 | tf_op jit(solution)/shard_map/all_gather | solution.py:59
  239.7 11.7 %cholesky.44 = f32[128,128]{1,0:T(8,128)S(1)} custom-call(f32[128,128]{1,0:T(8,128)S(1)} %fusion.178), custom_call_target="Cholesky" | custom-call | tf_op jit(solution)/shard_map/jit(cholesky)/cholesky | solution.py:120
  253.4 12.3 %all-gather.3 = f32[512,128]{1,0:T(8,128)S(1)} all-gather(f32[128,128]{1,0:T(8,128)S(1)} %fusion.2), channel_id=5, replica_groups=mesh['lat_0'=4,'lat_1'=4,'lon'=8,'ens'=2] {'lat_0'}, dimensions={0}, use_global_device_ids=true | all-gather | bytes 327680 | tf_op jit(solution)/shard_map/all_gather | solution.py:59
  265.6 9.8 %custom-call.8 = f32[1,128,128]{1,2,0:T(8,128)S(1)} custom-call(f32[1,128,128]{2,1,0:T(8,128)S(1)} %fusion.163), custom_call_target="InvertDiagBlocksLowerTriangular" | custom-call | tf_op jit(solution)/shard_map/jit(_cho_solve)/triangular_solve | solution.py:121
  275.5 12.3 %all-gather.4 = f32[512,128]{1,0:T(8,128)S(1)} all-gather(f32[128,128]{1,0:T(8,128)S(1)} %reduce_sum.148), channel_id=6, replica_groups=mesh['lat_0'=4,'lat_1'=4,'lon'=8,'ens'=2] {'lat_1'}, dimensions={0}, use_global_device_ids=true | all-gather | bytes 327680 | tf_op jit(solution)/shard_map/all_gather | solution.py:59
  287.7 25.6 %all-gather.5 = f32[1024,128]{1,0:T(8,128)S(1)} all-gather(f32[128,128]{1,0:T(8,128)S(1)} %reduce_sum.149), channel_id=7, replica_groups=mesh['lat_0'=4,'lat_1'=4,'lon'=8,'ens'=2] {'lon'}, dimensions={0}, use_global_device_ids=true | all-gather | bytes 589824 | tf_op jit(solution)/shard_map/all_gather | solution.py:59
  317.6 4.5 collective-permute-start.46
  341.8 6.4 %collective-permute-done.48 = f32[64,8,1]{2,1,0:T(8,128)S(1)} collective-permute-done((f32[64,8,1]{2,1,0:T(8,128)S(1)}, f32[64,8,1]{2,1,0:T(8,128)S(1)}, u32[]{:S(2)}, u32[]{:S(2)}) %collective-permute-start.48) | collective-permute-done | bytes 2080 | tf_op jit(solution)/shard_map/ppermute | solution.py:25
  359.8 5.4 collective-permute-done.52
  410.4 5.2 collective-permute-done.65
  459.5 6.0 collective-permute-start.82
  467.9 5.5 collective-permute-done.83
  480.2 12.4 %all-gather.6 = f32[512,128]{1,0:T(8,128)S(1)} all-gather(f32[128,128]{1,0:T(8,128)S(1)} %fusion.1), channel_id=8, replica_groups=mesh['lat_0'=4,'lat_1'=4,'lon'=8,'ens'=2] {'lat_0'}, dimensions={0}, use_global_device_ids=true | all-gather | bytes 327680 | tf_op jit(solution)/shard_map/all_gather | solution.py:59
  492.6 12.3 %all-gather.7 = f32[512,128]{1,0:T(8,128)S(1)} all-gather(f32[128,128]{1,0:T(8,128)S(1)} %reduce_sum.153), channel_id=9, replica_groups=mesh['lat_0'=4,'lat_1'=4,'lon'=8,'ens'=2] {'lat_1'}, dimensions={0}, use_global_device_ids=true | all-gather | bytes 327680 | tf_op jit(solution)/shard_map/all_gather | solution.py:59
  504.8 25.7 %all-gather.8 = f32[1024,128]{1,0:T(8,128)S(1)} all-gather(f32[128,128]{1,0:T(8,128)S(1)} %reduce_sum.154), channel_id=10, replica_groups=mesh['lat_0'=4,'lat_1'=4,'lon'=8,'ens'=2] {'lon'}, dimensions={0}, use_global_device_ids=true | all-gather | bytes 589824 | tf_op jit(solution)/shard_map/all_gather | solution.py:59
  530.9 11.7 %cholesky.55 = f32[128,128]{1,0:T(8,128)S(1)} custom-call(f32[128,128]{1,0:T(8,128)S(1)} %fusion.174), custom_call_target="Cholesky" | custom-call | tf_op jit(solution)/shard_map/jit(cholesky)/cholesky | solution.py:120
  544.7 12.3 %all-gather.9 = f32[512,128]{1,0:T(8,128)S(1)} all-gather(f32[128,128]{1,0:T(8,128)S(1)} %fusion), channel_id=11, replica_groups=mesh['lat_0'=4,'lat_1'=4,'lon'=8,'ens'=2] {'lat_0'}, dimensions={0}, use_global_device_ids=true | all-gather | bytes 327680 | tf_op jit(solution)/shard_map/all_gather | solution.py:59
  556.9 9.8 %custom-call.9 = f32[1,128,128]{1,2,0:T(8,128)S(1)} custom-call(f32[1,128,128]{2,1,0:T(8,128)S(1)} %fusion.164), custom_call_target="InvertDiagBlocksLowerTriangular" | custom-call | tf_op jit(solution)/shard_map/jit(_cho_solve)/triangular_solve | solution.py:121
  566.8 12.3 %all-gather.10 = f32[512,128]{1,0:T(8,128)S(1)} all-gather(f32[128,128]{1,0:T(8,128)S(1)} %reduce_sum.156), channel_id=12, replica_groups=mesh['lat_0'=4,'lat_1'=4,'lon'=8,'ens'=2] {'lat_1'}, dimensions={0}, use_global_device_ids=true | all-gather | bytes 327680 | tf_op jit(solution)/shard_map/all_gather | solution.py:59
  579.0 25.2 %all-gather.11 = f32[1024,128]{1,0:T(8,128)S(1)} all-gather(f32[128,128]{1,0:T(8,128)S(1)} %reduce_sum.157), channel_id=13, replica_groups=mesh['lat_0'=4,'lat_1'=4,'lon'=8,'ens'=2] {'lon'}, dimensions={0}, use_global_device_ids=true | all-gather | bytes 589824 | tf_op jit(solution)/shard_map/all_gather | solution.py:59
  (352 shorter events, 264.3 us)
Async XLA Ops:
  6.5 307.5 %all-gather.15.cloned.1.call-start = ((), (), s32[]{:S(2)}) async-start(), calls=%async_computation.1 | async-start | bytes 1572864 | tf_op jit(solution)/shard_map/all_gather | solution.py:156
  7.5 13.0 %collective-permute-start = (f32[64,8,1]{2,1,0:T(8,128)S(1)}, f32[64,8,1]{2,1,0:T(8,128)S(1)}, u32[]{:S(2)}, u32[]{:S(2)}) collective-permute-start(f32[64,8,1]{2,1,0:T(8,128)S(1)} %broadcast_in_dim.78), channel_id=1, source_target_pairs={{2,0},{4,2},{6,4},{8,6},{10,8},{12,10},{14,12},{0,14},{3,1},{5,3},... | collective-permute-start | bytes 6152 | tf_op jit(solution)/shard_map/ppermute | solution.py:25
  38.2 17.7 %collective-permute-start.10 = (f32[64,1,128]{2,1,0:T(1,128)S(1)}, f32[64,1,128]{2,1,0:T(1,128)S(1)}, u32[]{:S(2)}, u32[]{:S(2)}) collective-permute-start(f32[64,1,128]{2,1,0:T(1,128)S(1)} %get-tuple-element.108), channel_id=1, source_target_pairs={{16,0},{32,16},{48,32},{64,48},{80,64},{96,80},{112,96},{128,112},... | collective-permute-start | bytes 98312 | tf_op jit(solution)/shard_map/ppermute | solution.py:25
  44.3 11.7 %collective-permute-start.11 = (f32[64,1,128]{2,1,0:T(1,128)S(1)}, f32[64,1,128]{2,1,0:T(1,128)S(1)}, u32[]{:S(2)}, u32[]{:S(2)}) collective-permute-start(f32[64,1,128]{2,1,0:T(1,128)S(1)} %get-tuple-element.109), channel_id=1, source_target_pairs={{0,16},{16,32},{32,48},{48,64},{64,80},{80,96},{96,112},{112,128},... | collective-permute-start | bytes 98312 | tf_op jit(solution)/shard_map/ppermute | solution.py:24
  56.5 12.1 %collective-permute-start.13 = (f32[64,1,128]{2,1,0:T(1,128)S(1)}, f32[64,1,128]{2,1,0:T(1,128)S(1)}, u32[]{:S(2)}, u32[]{:S(2)}) collective-permute-start(f32[64,1,128]{2,1,0:T(1,128)S(1)} %get-tuple-element.102), channel_id=1, source_target_pairs={{0,16},{16,32},{32,48},{48,64},{64,80},{80,96},{96,112},{112,128},... | collective-permute-start | bytes 98312 | tf_op jit(solution)/shard_map/ppermute | solution.py:38
  56.6 12.0 %collective-permute-start.14 = (f32[64,1,128]{2,1,0:T(1,128)S(1)}, f32[64,1,128]{2,1,0:T(1,128)S(1)}, u32[]{:S(2)}, u32[]{:S(2)}) collective-permute-start(f32[64,1,128]{2,1,0:T(1,128)S(1)} %get-tuple-element.103), channel_id=1, source_target_pairs={{16,0},{32,16},{48,32},{64,48},{80,64},{96,80},{112,96},{128,112},... | collective-permute-start | bytes 98312 | tf_op jit(solution)/shard_map/ppermute | solution.py:39
  69.7 17.8 %collective-permute-start.18 = (f32[64,1,128]{2,1,0:T(1,128)S(1)}, f32[64,1,128]{2,1,0:T(1,128)S(1)}, u32[]{:S(2)}, u32[]{:S(2)}) collective-permute-start(f32[64,1,128]{2,1,0:T(1,128)S(1)} %get-tuple-element.100), channel_id=1, source_target_pairs={{16,0},{32,16},{48,32},{64,48},{80,64},{96,80},{112,96},{128,112},... | collective-permute-start | bytes 98312 | tf_op jit(solution)/shard_map/ppermute | solution.py:25
  73.6 13.9 %collective-permute-start.19 = (f32[64,1,128]{2,1,0:T(1,128)S(1)}, f32[64,1,128]{2,1,0:T(1,128)S(1)}, u32[]{:S(2)}, u32[]{:S(2)}) collective-permute-start(f32[64,1,128]{2,1,0:T(1,128)S(1)} %get-tuple-element.101), channel_id=1, source_target_pairs={{0,16},{16,32},{32,48},{48,64},{64,80},{80,96},{96,112},{112,128},... | collective-permute-start | bytes 98312 | tf_op jit(solution)/shard_map/ppermute | solution.py:24
  88.6 16.8 %collective-permute-start.20 = (f32[64,8,1]{2,1,0:T(8,128)S(1)}, f32[64,8,1]{2,1,0:T(8,128)S(1)}, u32[]{:S(2)}, u32[]{:S(2)}) collective-permute-start(f32[64,8,1]{2,1,0:T(8,128)S(1)} %get-tuple-element.96), channel_id=1, source_target_pairs={{0,2},{2,4},{4,6},{6,8},{8,10},{10,12},{12,14},{14,0},{1,3},{3,5},... | collective-permute-start | bytes 6152 | tf_op jit(solution)/shard_map/ppermute | solution.py:38
  88.6 16.8 %collective-permute-start.23 = (f32[64,8,1]{2,1,0:T(8,128)S(1)}, f32[64,8,1]{2,1,0:T(8,128)S(1)}, u32[]{:S(2)}, u32[]{:S(2)}) collective-permute-start(f32[64,8,1]{2,1,0:T(8,128)S(1)} %get-tuple-element.97), channel_id=1, source_target_pairs={{2,0},{4,2},{6,4},{8,6},{10,8},{12,10},{14,12},{0,14},{3,1},{5,3},... | collective-permute-start | bytes 6152 | tf_op jit(solution)/shard_map/ppermute | solution.py:39
  91.9 13.6 %collective-permute-start.21 = (f32[64,1,128]{2,1,0:T(1,128)}, f32[64,1,128]{2,1,0:T(1,128)S(1)}, u32[]{:S(2)}, u32[]{:S(2)}) collective-permute-start(f32[64,1,128]{2,1,0:T(1,128)} %get-tuple-element.94), channel_id=1, source_target_pairs={{0,16},{16,32},{32,48},{48,64},{64,80},{80,96},{96,112},{112,128},... | collective-permute-start | bytes 98312 | tf_op jit(solution)/shard_map/ppermute | solution.py:38
  92.2 13.3 %collective-permute-start.22 = (f32[64,1,128]{2,1,0:T(1,128)}, f32[64,1,128]{2,1,0:T(1,128)}, u32[]{:S(2)}, u32[]{:S(2)}) collective-permute-start(f32[64,1,128]{2,1,0:T(1,128)} %get-tuple-element.95), channel_id=1, source_target_pairs={{16,0},{32,16},{48,32},{64,48},{80,64},{96,80},{112,96},{128,112},... | collective-permute-start | bytes 98312 | tf_op jit(solution)/shard_map/ppermute | solution.py:39
  96.9 78.1 %all-to-all-start = ((f32[4,128,8]{2,0,1:T(4,128)}), f32[4,128,8]{2,0,1:T(4,128)S(1)}, u32[]{:S(2)}, u32[]{:S(2)}) async-start(f32[4,128,8]{2,0,1:T(4,128)} %copy.90), calls=%async_computation | async-start | bytes 524288 | tf_op jit(solution)/shard_map/all_to_all | solution.py:53
  105.4 499.5 %all-gather.17.cloned.1.call-start = ((), (), s32[]{:S(2)}) async-start(), calls=%async_computation.2 | async-start | bytes 1572864 | tf_op jit(solution)/shard_map/all_gather | solution.py:156
  164.0 11.3 %collective-permute-start.40 = (f32[64,8,1]{2,1,0:T(8,128)S(1)}, f32[64,8,1]{2,1,0:T(8,128)S(1)}, u32[]{:S(2)}, u32[]{:S(2)}) collective-permute-start(f32[64,8,1]{2,1,0:T(8,128)S(1)} %get-tuple-element.74), channel_id=1, source_target_pairs={{2,0},{4,2},{6,4},{8,6},{10,8},{12,10},{14,12},{0,14},{3,1},{5,3},... | collective-permute-start | bytes 6152 | tf_op jit(solution)/shard_map/ppermute | solution.py:25
  317.5 15.1 %collective-permute-start.45 = (f32[64,1,128]{2,1,0:T(1,128)S(1)}, f32[64,1,128]{2,1,0:T(1,128)S(1)}, u32[]{:S(2)}, u32[]{:S(2)}) collective-permute-start(f32[64,1,128]{2,1,0:T(1,128)S(1)} %get-tuple-element.70), channel_id=1, source_target_pairs={{0,16},{16,32},{32,48},{48,64},{64,80},{80,96},{96,112},{112,128},... | collective-permute-start | bytes 98312 | tf_op jit(solution)/shard_map/ppermute | solution.py:38
  317.6 15.0 %collective-permute-start.46 = (f32[64,1,128]{2,1,0:T(1,128)S(1)}, f32[64,1,128]{2,1,0:T(1,128)S(1)}, u32[]{:S(2)}, u32[]{:S(2)}) collective-permute-start(f32[64,1,128]{2,1,0:T(1,128)S(1)} %get-tuple-element.71), channel_id=1, source_target_pairs={{16,0},{32,16},{48,32},{64,48},{80,64},{96,80},{112,96},{128,112},... | collective-permute-start | bytes 98312 | tf_op jit(solution)/shard_map/ppermute | solution.py:39
  333.7 17.9 %collective-permute-start.50 = (f32[64,1,128]{2,1,0:T(1,128)S(1)}, f32[64,1,128]{2,1,0:T(1,128)S(1)}, u32[]{:S(2)}, u32[]{:S(2)}) collective-permute-start(f32[64,1,128]{2,1,0:T(1,128)S(1)} %get-tuple-element.68), channel_id=1, source_target_pairs={{16,0},{32,16},{48,32},{64,48},{80,64},{96,80},{112,96},{128,112},... | collective-permute-start | bytes 98312 | tf_op jit(solution)/shard_map/ppermute | solution.py:25
  335.7 16.0 %collective-permute-start.51 = (f32[64,1,128]{2,1,0:T(1,128)S(1)}, f32[64,1,128]{2,1,0:T(1,128)S(1)}, u32[]{:S(2)}, u32[]{:S(2)}) collective-permute-start(f32[64,1,128]{2,1,0:T(1,128)S(1)} %get-tuple-element.69), channel_id=1, source_target_pairs={{0,16},{16,32},{32,48},{48,64},{64,80},{80,96},{96,112},{112,128},... | collective-permute-start | bytes 98312 | tf_op jit(solution)/shard_map/ppermute | solution.py:24
  352.2 13.0 %collective-permute-start.53 = (f32[64,1,128]{2,1,0:T(1,128)S(1)}, f32[64,1,128]{2,1,0:T(1,128)S(1)}, u32[]{:S(2)}, u32[]{:S(2)}) collective-permute-start(f32[64,1,128]{2,1,0:T(1,128)S(1)} %get-tuple-element.62), channel_id=1, source_target_pairs={{0,16},{16,32},{32,48},{48,64},{64,80},{80,96},{96,112},{112,128},... | collective-permute-start | bytes 98312 | tf_op jit(solution)/shard_map/ppermute | solution.py:38
  352.6 12.7 %collective-permute-start.54 = (f32[64,1,128]{2,1,0:T(1,128)S(1)}, f32[64,1,128]{2,1,0:T(1,128)S(1)}, u32[]{:S(2)}, u32[]{:S(2)}) collective-permute-start(f32[64,1,128]{2,1,0:T(1,128)S(1)} %get-tuple-element.63), channel_id=1, source_target_pairs={{16,0},{32,16},{48,32},{64,48},{80,64},{96,80},{112,96},{128,112},... | collective-permute-start | bytes 98312 | tf_op jit(solution)/shard_map/ppermute | solution.py:39
  366.4 16.6 %collective-permute-start.58 = (f32[64,1,128]{2,1,0:T(1,128)S(1)}, f32[64,1,128]{2,1,0:T(1,128)S(1)}, u32[]{:S(2)}, u32[]{:S(2)}) collective-permute-start(f32[64,1,128]{2,1,0:T(1,128)S(1)} %get-tuple-element.60), channel_id=1, source_target_pairs={{16,0},{32,16},{48,32},{64,48},{80,64},{96,80},{112,96},{128,112},... | collective-permute-start | bytes 98312 | tf_op jit(solution)/shard_map/ppermute | solution.py:25
  368.6 14.4 %collective-permute-start.59 = (f32[64,1,128]{2,1,0:T(1,128)S(1)}, f32[64,1,128]{2,1,0:T(1,128)S(1)}, u32[]{:S(2)}, u32[]{:S(2)}) collective-permute-start(f32[64,1,128]{2,1,0:T(1,128)S(1)} %get-tuple-element.61), channel_id=1, source_target_pairs={{0,16},{16,32},{32,48},{48,64},{64,80},{80,96},{96,112},{112,128},... | collective-permute-start | bytes 98312 | tf_op jit(solution)/shard_map/ppermute | solution.py:24
  383.3 12.2 %collective-permute-start.61 = (f32[64,1,128]{2,1,0:T(1,128)S(1)}, f32[64,1,128]{2,1,0:T(1,128)S(1)}, u32[]{:S(2)}, u32[]{:S(2)}) collective-permute-start(f32[64,1,128]{2,1,0:T(1,128)S(1)} %get-tuple-element.54), channel_id=1, source_target_pairs={{0,16},{16,32},{32,48},{48,64},{64,80},{80,96},{96,112},{112,128},... | collective-permute-start | bytes 98312 | tf_op jit(solution)/shard_map/ppermute | solution.py:38
  383.6 11.9 %collective-permute-start.62 = (f32[64,1,128]{2,1,0:T(1,128)S(1)}, f32[64,1,128]{2,1,0:T(1,128)S(1)}, u32[]{:S(2)}, u32[]{:S(2)}) collective-permute-start(f32[64,1,128]{2,1,0:T(1,128)S(1)} %get-tuple-element.55), channel_id=1, source_target_pairs={{16,0},{32,16},{48,32},{64,48},{80,64},{96,80},{112,96},{128,112},... | collective-permute-start | bytes 98312 | tf_op jit(solution)/shard_map/ppermute | solution.py:39
  396.7 18.9 %collective-permute-start.66 = (f32[64,1,128]{2,1,0:T(1,128)S(1)}, f32[64,1,128]{2,1,0:T(1,128)S(1)}, u32[]{:S(2)}, u32[]{:S(2)}) collective-permute-start(f32[64,1,128]{2,1,0:T(1,128)S(1)} %get-tuple-element.52), channel_id=1, source_target_pairs={{16,0},{32,16},{48,32},{64,48},{80,64},{96,80},{112,96},{128,112},... | collective-permute-start | bytes 98312 | tf_op jit(solution)/shard_map/ppermute | solution.py:25
  398.9 16.7 %collective-permute-start.67 = (f32[64,1,128]{2,1,0:T(1,128)S(1)}, f32[64,1,128]{2,1,0:T(1,128)S(1)}, u32[]{:S(2)}, u32[]{:S(2)}) collective-permute-start(f32[64,1,128]{2,1,0:T(1,128)S(1)} %get-tuple-element.53), channel_id=1, source_target_pairs={{0,16},{16,32},{32,48},{48,64},{64,80},{80,96},{96,112},{112,128},... | collective-permute-start | bytes 98312 | tf_op jit(solution)/shard_map/ppermute | solution.py:24
  415.9 12.0 %collective-permute-start.69 = (f32[64,1,128]{2,1,0:T(1,128)S(1)}, f32[64,1,128]{2,1,0:T(1,128)S(1)}, u32[]{:S(2)}, u32[]{:S(2)}) collective-permute-start(f32[64,1,128]{2,1,0:T(1,128)S(1)} %get-tuple-element.46), channel_id=1, source_target_pairs={{0,16},{16,32},{32,48},{48,64},{64,80},{80,96},{96,112},{112,128},... | collective-permute-start | bytes 98312 | tf_op jit(solution)/shard_map/ppermute | solution.py:38
  416.3 11.6 %collective-permute-start.70 = (f32[64,1,128]{2,1,0:T(1,128)S(1)}, f32[64,1,128]{2,1,0:T(1,128)S(1)}, u32[]{:S(2)}, u32[]{:S(2)}) collective-permute-start(f32[64,1,128]{2,1,0:T(1,128)S(1)} %get-tuple-element.47), channel_id=1, source_target_pairs={{16,0},{32,16},{48,32},{64,48},{80,64},{96,80},{112,96},{128,112},... | collective-permute-start | bytes 98312 | tf_op jit(solution)/shard_map/ppermute | solution.py:39
  429.1 16.9 %collective-permute-start.74 = (f32[64,1,128]{2,1,0:T(1,128)S(1)}, f32[64,1,128]{2,1,0:T(1,128)S(1)}, u32[]{:S(2)}, u32[]{:S(2)}) collective-permute-start(f32[64,1,128]{2,1,0:T(1,128)S(1)} %get-tuple-element.44), channel_id=1, source_target_pairs={{16,0},{32,16},{48,32},{64,48},{80,64},{96,80},{112,96},{128,112},... | collective-permute-start | bytes 98312 | tf_op jit(solution)/shard_map/ppermute | solution.py:25
  432.9 13.1 %collective-permute-start.75 = (f32[64,1,128]{2,1,0:T(1,128)S(1)}, f32[64,1,128]{2,1,0:T(1,128)S(1)}, u32[]{:S(2)}, u32[]{:S(2)}) collective-permute-start(f32[64,1,128]{2,1,0:T(1,128)S(1)} %get-tuple-element.45), channel_id=1, source_target_pairs={{0,16},{16,32},{32,48},{48,64},{64,80},{80,96},{96,112},{112,128},... | collective-permute-start | bytes 98312 | tf_op jit(solution)/shard_map/ppermute | solution.py:24
  457.3 10.6 %collective-permute-start.80 = (f32[64,8,1]{2,1,0:T(8,128)S(1)}, f32[64,8,1]{2,1,0:T(8,128)S(1)}, u32[]{:S(2)}, u32[]{:S(2)}) collective-permute-start(f32[64,8,1]{2,1,0:T(8,128)S(1)} %get-tuple-element.34), channel_id=1, source_target_pairs={{2,0},{4,2},{6,4},{8,6},{10,8},{12,10},{14,12},{0,14},{3,1},{5,3},... | collective-permute-start | bytes 6152 | tf_op jit(solution)/shard_map/ppermute | solution.py:25
  (69 other events, 710.0 us)
Sparse Core Ops, SparseCore 0:
  79.4 14.2 all-gather.14
  468.0 15.9 all-gather.16
